TPU v7x, 32 devices: a whole 2x2x4 slice. The times are simulated.
32 devices in a mesh: gz: 8 (over y, x, core), gy: 4 (over z).
Axes of the slice: x: 2, y: 2, z: 4, core: 2. Of those that a mesh axis runs over, the one named last changes fastest.
Arguments:
- velocity: bfloat16 [3, 128, 64, 128], P(None, 'gz', 'gy'), may hold values from -6 to 6
- lag_table: int32 [5, 3], replicated, may hold values from -64 to 64, as said below
- filter_index: int32 [5, 16], replicated, may hold values from 0 to 31
- filter_weights: float32 [3, 32], replicated, may hold values from -4 to 4
Outputs:
- transfer: float32 [128, 64, 128], P('gz', 'gy')
Inputs may be any that keep to these rules, and one draw needn't show every extreme that they name: `lag_table`: column 0 is a base x-offset from 0 to 48, column 1 a y lag from -4 to 4, column 2 a z lag from -64 to 64; one lag has z lag exactly 64 and another exactly -64.
All inputs are finite; a program needn't handle non-finite values.
Results may differ from a plain program's by a relative error of at most 0.0004.
Values may be sent and summed in bfloat16 or wider, within the bound.
A program may use at most 64 MiB of HBM per device.

v0:
```python
import jax
import jax.numpy as jnp
from jax import lax
from jax.sharding import PartitionSpec as P

NLAG = 5
NOFF = 16
YREACH = 4


def extended_2(block, sides, width):
    for axis, dim in sides:
        count = lax.axis_size(axis)
        forward = [(i, i + 1) for i in range(count - 1)]
        forward.append((count - 1, 0))
        backward = [(target, source) for source, target in forward]
        low = lax.ppermute(
            lax.slice_in_dim(block, block.shape[dim] - width, None, axis=dim), axis, forward
        )
        high = lax.ppermute(lax.slice_in_dim(block, 0, width, axis=dim), axis, backward)
        block = jnp.concatenate([low, block, high], axis=dim)
    return block


def from_behind(x, axis, by):
    peers = lax.axis_size(axis)
    return lax.ppermute(x, axis, [(i, (i + by) % peers) for i in range(peers)])


def cubic_sum(shifted, base_field, start, indices, filter_weights, total):
    length = base_field.shape[3]
    doubled = jnp.concatenate([shifted, shifted], axis=3)
    choices_index = jnp.arange(filter_weights.shape[1], dtype=jnp.int32)
    for offset in range(NOFF):
        moved = lax.dynamic_slice_in_dim(doubled, start + offset, length, axis=3)
        diff = moved.astype(jnp.float32) - base_field
        pick = (choices_index == indices[offset]).astype(jnp.float32)
        gradient = jnp.sum(filter_weights * pick[None, :], axis=1)
        along = gradient[0] * diff[0] + gradient[1] * diff[1] + gradient[2] * diff[2]
        energy = diff[0] * diff[0] + diff[1] * diff[1] + diff[2] * diff[2]
        total = total + along * energy
    return total


def per_device(velocity, lag_table, filter_index, filter_weights):
    planes = velocity.shape[1]
    rows = velocity.shape[2]
    length = velocity.shape[3]
    count = lax.axis_size("gz")
    levels = (count - 1).bit_length()
    zero = jnp.int32(0)
    widened = extended_2(velocity, (("gy", 2),), YREACH)
    following = from_behind(widened, "gz", -1)
    extended = jnp.concatenate([widened, following], axis=1)
    base_field = velocity.astype(jnp.float32)
    blocks = []
    distances = []
    remainders = []
    for lag in range(NLAG):
        lag_y = lag_table[lag, 1]
        lag_z = lag_table[lag, 2]
        whole = jnp.floor_divide(lag_z, planes)
        rest = lag_z - whole * planes
        distances.append(jnp.mod(whole, count))
        remainders.append(rest)
        block = lax.dynamic_slice(
            extended, (zero, zero, YREACH + lag_y, zero), (3, 2 * planes, rows, length)
        )
        blocks.append(block)
    stacked = jnp.stack(blocks)
    hop_vector = jnp.stack(distances)
    for level in range(levels):
        moved = from_behind(stacked, "gz", -(1 << level))
        take = jnp.bitwise_and(jnp.right_shift(hop_vector, level), 1) == 1
        stacked = jnp.where(take[:, None, None, None, None], moved, stacked)
    blocks = [stacked[lag] for lag in range(NLAG)]
    total = jnp.zeros((planes, rows, length), jnp.float32)
    for lag in range(NLAG):
        shifted = blocks[lag]
        shifted = lax.dynamic_slice(
            shifted, (zero, remainders[lag], zero, zero), (3, planes, rows, length)
        )
        start = lag_table[lag, 0]
        total = cubic_sum(shifted, base_field, start, filter_index[lag], filter_weights, total)
    return total * (0.25 / (NLAG * NOFF))


def solution(mesh):
    in_specs = (P(None, "gz", "gy", None), P(), P(), P())
    out_specs = P("gz", "gy", None)
    return jax.shard_map(
        per_device, mesh=mesh, in_specs=in_specs, out_specs=out_specs, check_vma=False
    )
```

profile of v0, /device:TPU:0, one launch (start us, length us, event | category | flops | bytes accessed | tf_op | source)
XLA Modules:
  0.0 442.9 jit_solution(11188396115455374024)
XLA Ops:
  1.0 3.1 collective-permute-start
  4.1 2.1 collective-permute-start.1
  6.2 2.1 fusion.85
  8.3 2.1 fusion.86
  10.4 1.5 fusion.87
  11.9 2.1 fusion.83
  14.0 2.1 fusion.84
  16.1 1.9 fusion.88
  69.6 1.7 collective-permute-start.2
  73.2 2.3 collective-permute-done.2
  75.5 1.1 pad_maximum_fusion
  77.6 2.9 collective-permute-start.3
  102.7 1.8 broadcast_select_fusion
  115.8 34.1 %collective-permute-done.4 = bf16[5,3,32,16,128]{4,3,2,1,0:T(8,128)(2,1)S(1)} collective-permute-done((bf16[5,3,32,16,128]{4,3,2,1,0:T(8,128)(2,1)S(1)}, bf16[5,3,32,16,128]{4,3,2,1,0:T(8,128)(2,1)S(1)}, u32[]{:S(2)}, u32[]{:S(2)}) %collective-permute-start.4) | collective-permute-done | bytes 1966112 | tf_op jit(solution)/shard_map/ppermute | solution.py:27
  268.1 1.8 broadcast_select_fusion.2
  270.9 1.1 convert_subtract_fusion.78
  272.0 1.8 add_multiply_fusion.34
  273.8 1.1 convert_subtract_fusion.79
  274.9 1.9 add_multiply_fusion.29
  276.9 1.9 add_multiply_fusion.30
  278.8 1.9 add_multiply_fusion.31
  280.7 1.8 add_multiply_fusion.32
  282.5 1.9 add_multiply_fusion.33
  284.5 1.1 convert_subtract_fusion.56
  285.6 1.9 add_multiply_fusion.20
  287.5 1.9 add_multiply_fusion.21
  289.4 1.9 add_multiply_fusion.22
  291.3 2.0 add_multiply_fusion.23
  293.3 1.9 add_multiply_fusion.24
  295.2 1.9 add_multiply_fusion.35
  297.1 2.0 add_multiply_fusion.36
  299.1 1.9 add_multiply_fusion.37
  301.0 1.9 add_multiply_fusion.38
  302.9 1.8 add_multiply_fusion.39
  305.4 2.0 add_multiply_fusion.25
  307.5 1.8 add_multiply_fusion.26
  309.3 2.0 add_multiply_fusion.27
  311.3 1.9 add_multiply_fusion.28
  313.2 2.0 add_multiply_fusion.40
  315.2 1.1 convert_subtract_fusion.55
  316.4 1.7 add_multiply_fusion.19
  321.0 1.1 convert_subtract_fusion.25
  322.1 1.1 convert_subtract_fusion.9
  323.3 1.1 convert_subtract_fusion.31
  324.4 1.1 convert_subtract_fusion.15
  325.5 1.1 convert_subtract_fusion.41
  326.6 1.1 convert_subtract_fusion.47
  327.7 115.2 %fusion.80 = f32[16,16,128]{2,1,0:T(8,128)} fusion(f32[1,16,16,128]{3,2,1,0:T(8,128)S(1)} %add_multiply_fusion.19, f32[1,16,16,128]{3,2,1,0:T(8,128)S(1)} %add_multiply_fusion.20, f32[1,16,16,128]{3,2,1,0:T(8,128)S(1)} %add_multiply_fusion.21, f32[1,16,16,128]{3,2,1,0:T(8,128)S(1)} %add_multiply_fusion.22, f32[1,16,16,128]{3,2,1,0:T(8,128)S(1)} %add_multiply_fusion.23, ...), kind=kLoop, calls=%fused_computation.336 | loop fusion | flops 23527424 | bytes 25821880 | tf_op jit(solution)/shard_map/mul | solution.py:85
  (154 shorter events, 87.2 us)
Async XLA Ops:
  1.0 67.5 %collective-permute-start = (bf16[3,16,4,128]{3,2,1,0:T(4,128)(2,1)S(1)}, bf16[3,16,4,128]{3,2,1,0:T(4,128)(2,1)S(1)}, u32[]{:S(2)}, u32[]{:S(2)}) collective-permute-start(bf16[3,16,4,128]{3,2,1,0:T(4,128)(2,1)S(1)} %get-tuple-element.170), channel_id=1, source_target_pairs={{0,1},{1,2},{2,3},{3,0},{4,5},{5,6},{6,7},{7,4},{8,9},{9,10},{10,1... | collective-permute-start | bytes 147464 | tf_op jit(solution)/shard_map/ppermute | solution.py:17
  4.1 64.4 %collective-permute-start.1 = (bf16[3,16,4,128]{3,2,1,0:T(4,128)(2,1)S(1)}, bf16[3,16,4,128]{3,2,1,0:T(4,128)(2,1)S(1)}, u32[]{:S(2)}, u32[]{:S(2)}) collective-permute-start(bf16[3,16,4,128]{3,2,1,0:T(4,128)(2,1)S(1)} %get-tuple-element.171), channel_id=1, source_target_pairs={{1,0},{2,1},{3,2},{0,3},{5,4},{6,5},{7,6},{4,7},{9,8},{10,9},{11,1... | collective-permute-start | bytes 147464 | tf_op jit(solution)/shard_map/ppermute | solution.py:20
  69.6 5.9 %collective-permute-start.2 = (bf16[3,16,24,128]{3,2,1,0:T(8,128)(2,1)S(1)}, bf16[3,16,24,128]{3,2,1,0:T(8,128)(2,1)S(1)}, u32[]{:S(2)}, u32[]{:S(2)}) collective-permute-start(bf16[3,16,24,128]{3,2,1,0:T(8,128)(2,1)S(1)} %pad_maximum_fusion.1), channel_id=1, source_target_pairs={{0,28},{4,0},{8,4},{12,8},{16,12},{20,16},{24,20},{28,24},{1,29},{... | collective-permute-start | bytes 884744 | tf_op jit(solution)/shard_map/ppermute | solution.py:27
  76.6 20.1 %copy-start.1 = (f32[3,32]{1,0:T(4,128)S(1)}, f32[3,32]{1,0:T(4,128)}, u32[]{:S(2)}) copy-start(f32[3,32]{1,0:T(4,128)} %param.7) | copy-start | bytes 1156
  77.6 25.1 %collective-permute-start.3 = (bf16[5,3,32,16,128]{4,3,2,1,0:T(8,128)(2,1)S(1)}, bf16[5,3,32,16,128]{4,3,2,1,0:T(8,128)(2,1)}, u32[]{:S(2)}, u32[]{:S(2)}) collective-permute-start(bf16[5,3,32,16,128]{4,3,2,1,0:T(8,128)(2,1)S(1)} %bitcast_dynamic-update-slice_fusion), channel_id=1, source_target_pairs={{0,28},{4,0},{8,4},{12,8},{16,12},{20,16},{24,20},{28,24},{1,29},{... | collective-permute-start | bytes 5898248 | tf_op jit(solution)/shard_map/ppermute | solution.py:27
  104.5 45.5 %collective-permute-start.4 = (bf16[5,3,32,16,128]{4,3,2,1,0:T(8,128)(2,1)S(1)}, bf16[5,3,32,16,128]{4,3,2,1,0:T(8,128)(2,1)S(1)}, u32[]{:S(2)}, u32[]{:S(2)}) collective-permute-start(bf16[5,3,32,16,128]{4,3,2,1,0:T(8,128)(2,1)S(1)} %broadcast_select_fusion), channel_id=1, source_target_pairs={{0,24},{4,28},{8,0},{12,4},{16,8},{20,12},{24,16},{28,20},{1,25},{... | collective-permute-start | bytes 5898248 | tf_op jit(solution)/shard_map/ppermute | solution.py:27
  150.2 117.9 %collective-permute-start.5 = (bf16[5,3,32,16,128]{4,3,2,1,0:T(8,128)(2,1)S(1)}, bf16[5,3,32,16,128]{4,3,2,1,0:T(8,128)(2,1)}, u32[]{:S(2)}, u32[]{:S(2)}) collective-permute-start(bf16[5,3,32,16,128]{4,3,2,1,0:T(8,128)(2,1)S(1)} %broadcast_select_fusion.1), channel_id=1, source_target_pairs={{0,16},{4,20},{8,24},{12,28},{16,0},{20,4},{24,8},{28,12},{1,17},{... | collective-permute-start | bytes 5898248 | tf_op jit(solution)/shard_map/ppermute | solution.py:27
  270.0 0.9 copy-start
where the time goes:
time: 448 us; the launch traced here: 443 us
  other arithmetic  230 us (51%)
  between operations  125 us (28%)
  local copies, waits for them, and re-layouts  41.1 us (9%)
  waiting for transfers between devices  36.5 us (8%)
  starting transfers between devices  10.5 us (2%)
    mul x1, other arithmetic, per_device(): return total * (0.25 / (NLAG * NOFF))  115 us
    convert_element_type x80, other arithmetic, cubic_sum(): pick = (choices_index == indices[offset]).astype(jnp.float32)  50.2 us
    mul x22, other arithmetic, cubic_sum(): total = total + along * energy  41.9 us
    ppermute x4, waiting for transfers between devices, from_behind(): return lax.ppermute(x, axis, [(i, (i + by) % peers) for i in range(peers)])  36.5 us
    slice x40, local copies, waits for them, and re-layouts, cubic_sum(): gradient[0] * diff[0] + gradient[1] * diff[1] + gradient[2] * diff[2]  26.4 us
    sub x15, other arithmetic, cubic_sum(): diff = moved.astype(jnp.float32) - base_field  14.7 us
    slice x5, local copies, waits for them, and re-layouts, cubic_sum(): pick = (choices_index == indices[offset]).astype(jnp.float32)  9.88 us
  transfers between devices with their start and end apart: 6, of which 2 were waited for; matrix products, arithmetic and copies ran while one was open for 20% of the time, Pallas kernels for 0%

commit v1 on v0

v1 whole, which is shorter than its diff:
```python
import functools

import jax
import jax.numpy as jnp
from jax import lax
from jax.experimental import pallas as pl
from jax.experimental.pallas import tpu as pltpu
from jax.sharding import PartitionSpec as P

NLAG = 5
NOFF = 16
REACH = 64
TILE = 8
MESH = pl.DeviceIdType.MESH


def kernel(
    pairs, reach, columns, lag_ref, index_ref, weight_ref, vel_ref, out_ref,
    field, base, window, own_sem, send_sem, recv_sem, share_send, share_recv
):
    planes, tiles = vel_ref.shape[1], vel_ref.shape[2]
    length = vel_ref.shape[4]
    slots = field.shape[0]
    last = tiles + 1
    home = reach % pairs
    me = lax.axis_index("gz")
    col = lax.axis_index("gy")
    pair = me // 2
    side = lax.rem(me, 2)
    up = lax.rem(col + 1, columns)
    down = lax.rem(col + columns - 1, columns)
    partner = (pair * 2 + 1 - side, col)
    others = [s for s in range(slots) if s != home]
    others.sort(key=lambda s: -abs(s - reach))

    def peer(slot):
        return (lax.rem(pair + pairs + reach - slot, pairs) * 2 + side, col)

    own = [
        pltpu.make_async_copy(vel_ref.at[:, :, t], field.at[home, side, t + 1], own_sem.at[t])
        for t in range(tiles)
    ]
    for copy in own:
        copy.start()

    barrier = pltpu.get_barrier_semaphore()
    greeted = [peer(s) for s in others] + [partner, (me, up), (me, down)]
    for device in greeted:
        pl.semaphore_signal(barrier, inc=1, device_id=device, device_id_type=MESH)
    pl.semaphore_wait(barrier, len(greeted))

    def direct(src, slot, tile, device):
        return pltpu.make_async_remote_copy(
            src_ref=src,
            dst_ref=field.at[slot, side, tile],
            send_sem=send_sem.at[slot, tile],
            recv_sem=recv_sem.at[slot, tile],
            device_id=device,
            device_id_type=MESH,
        )

    def share(src, slot, tile):
        return pltpu.make_async_remote_copy(
            src_ref=src,
            dst_ref=field.at[slot, side, tile],
            send_sem=share_send.at[slot, tile],
            recv_sem=share_recv.at[slot, tile],
            device_id=partner,
            device_id_type=MESH,
        )

    def incoming(slot, tile):
        return pltpu.make_async_remote_copy(
            src_ref=field.at[slot, 1 - side, tile],
            dst_ref=field.at[slot, 1 - side, tile],
            send_sem=share_send.at[slot, tile],
            recv_sem=share_recv.at[slot, tile],
            device_id=partner,
            device_id_type=MESH,
        )

    started = []

    def go(copy):
        copy.start()
        started.append(copy)
        return copy

    mains = {}
    halos = {}
    for s in others:
        for t in range(tiles):
            mains[s, t] = go(direct(vel_ref.at[:, :, t], s, t + 1, peer(s)))
    halos[home, 0] = go(direct(vel_ref.at[:, :, tiles - 1], home, 0, (me, up)))
    halos[home, last] = go(direct(vel_ref.at[:, :, 0], home, last, (me, down)))
    for t in range(tiles):
        go(share(vel_ref.at[:, :, t], home, t + 1))

    for copy in own:
        copy.wait()

    def fill_base(z, _):
        for c in range(3):
            for t in range(tiles):
                base[c, z, t * TILE:(t + 1) * TILE, :] = field[home, side, t + 1, c, z].astype(jnp.float32)
        for t in range(tiles):
            out_ref[z, t * TILE:(t + 1) * TILE, :] = jnp.zeros((TILE, length), jnp.float32)
        return 0

    lax.fori_loop(0, planes, fill_base, 0)

    def add_lag(lag):
        start = lag_ref[lag, 0]
        lag_y = lag_ref[lag, 1]
        turn = lax.rem(length - start, length)

        def step(z, _):
            spots = [(z * 2 + dz, t) for dz in range(2) for t in range(tiles)]
            centre = [[base[c, zz, t * TILE:(t + 1) * TILE, :] for c in range(3)] for zz, t in spots]
            moved = [
                [
                    pltpu.roll(window[c, zz, pl.ds(TILE + lag_y + t * TILE, TILE), :], turn, 1)
                    for c in range(3)
                ]
                for zz, t in spots
            ]
            total = [out_ref[zz, t * TILE:(t + 1) * TILE, :] for zz, t in spots]
            for k in range(NOFF):
                row = index_ref[lag, k]
                g = [weight_ref[c, row] for c in range(3)]
                for i in range(len(spots)):
                    diff = [
                        (pltpu.roll(moved[i][c], length - k, 1) if k else moved[i][c]) - centre[i][c]
                        for c in range(3)
                    ]
                    along = g[0] * diff[0] + g[1] * diff[1] + g[2] * diff[2]
                    energy = diff[0] * diff[0] + diff[1] * diff[1] + diff[2] * diff[2]
                    total[i] = total[i] + along * energy
            for i, (zz, t) in enumerate(spots):
                out_ref[zz, t * TILE:(t + 1) * TILE, :] = total[i]
            return 0

        lax.fori_loop(0, planes // 2, step, 0)

    def end_lag(lag, slot):
        def load(z, _):
            for c in range(3):
                for t in range(last + 1):
                    window[c, z, t * TILE:(t + 1) * TILE, :] = field[slot, side, t, c, z].astype(jnp.float32)
            return 0

        lax.fori_loop(0, planes, load, 0)
        add_lag(lag)

    def any_lag(lag):
        lag_z = lag_ref[lag, 2]

        def load(z, _):
            away = lag_z + z + 2 * reach * planes
            block = lax.div(away, planes) + side
            plane = lax.rem(away, planes)
            slot = lax.rem(lax.div(block, 2), pairs)
            parity = lax.rem(block, 2)
            for c in range(3):
                for t in range(last + 1):
                    window[c, z, t * TILE:(t + 1) * TILE, :] = field[slot, parity, t, c, plane].astype(jnp.float32)
            return 0

        lax.fori_loop(0, planes, load, 0)
        add_lag(lag)

    for s in others:
        for t in range(tiles):
            mains[s, t].wait_recv()
            if t == 0:
                halos[s, last] = go(direct(field.at[s, side, 1], s, last, (me, down)))
            if t == tiles - 1:
                halos[s, 0] = go(direct(field.at[s, side, tiles], s, 0, (me, up)))
            go(share(field.at[s, side, t + 1], s, t + 1))
        if s == others[0]:
            for edge in (0, last):
                halos[home, edge].wait_recv()
                go(share(field.at[home, side, edge], home, edge))
    for s in others:
        for edge in (last, 0):
            halos[s, edge].wait_recv()
            go(share(field.at[s, side, edge], s, edge))

    plus = jnp.int32(0)
    minus = jnp.int32(0)
    for lag in range(NLAG - 1, -1, -1):
        plus = jnp.where(lag_ref[lag, 2] == REACH, lag, plus)
        minus = jnp.where(lag_ref[lag, 2] == -REACH, lag, minus)
    end_lag(plus, (2 * reach) % pairs)
    end_lag(minus, 0)

    for s in [home] + others:
        for t in range(last + 1):
            incoming(s, t).wait_recv()

    low = jnp.minimum(plus, minus)
    high = jnp.maximum(plus, minus)

    def rest(j, _):
        lag = j + jnp.where(j >= low, 1, 0)
        lag = lag + jnp.where(lag >= high, 1, 0)
        any_lag(lag)
        return 0

    lax.fori_loop(0, NLAG - 2, rest, 0)

    def finish(z, _):
        out_ref[z] = out_ref[z] * (0.25 / (NLAG * NOFF))
        return 0

    lax.fori_loop(0, planes, finish, 0)
    for copy in started:
        copy.wait_send()


def solution(mesh):
    count = mesh.shape["gz"]
    columns = mesh.shape["gy"]
    pairs = count // 2

    def per_device(velocity, lag_table, filter_index, filter_weights):
        parts, planes, rows, length = velocity.shape
        reach = REACH // (2 * planes)
        tiles = rows // TILE
        slots = min(pairs, 2 * reach + 1)
        blocks = velocity.reshape(parts, planes, tiles, TILE, length)
        smem = pl.BlockSpec(memory_space=pltpu.SMEM)
        return pl.pallas_call(
            functools.partial(kernel, pairs, reach, columns),
            out_shape=jax.ShapeDtypeStruct((planes, rows, length), jnp.float32),
            in_specs=[smem, smem, smem, pl.BlockSpec(memory_space=pl.ANY)],
            out_specs=pl.BlockSpec(memory_space=pltpu.VMEM),
            scratch_shapes=[
                pltpu.VMEM((slots, 2, tiles + 2, parts, planes, TILE, length), jnp.bfloat16),
                pltpu.VMEM((parts, planes, rows, length), jnp.float32),
                pltpu.VMEM((parts, planes, rows + 2 * TILE, length), jnp.float32),
                pltpu.SemaphoreType.DMA((tiles,)),
                pltpu.SemaphoreType.DMA((slots, tiles + 2)),
                pltpu.SemaphoreType.DMA((slots, tiles + 2)),
                pltpu.SemaphoreType.DMA((slots, tiles + 2)),
                pltpu.SemaphoreType.DMA((slots, tiles + 2)),
            ],
            compiler_params=pltpu.CompilerParams(collective_id=0, has_side_effects=True),
        )(lag_table, filter_index, filter_weights, blocks)

    return jax.shard_map(
        per_device,
        mesh=mesh,
        in_specs=(P(None, "gz", "gy", None), P(), P(), P()),
        out_specs=P("gz", "gy", None),
        check_vma=False,
    )
```

time: 448 us -> 48.7 us (0.11); the launches traced: 443 us -> 48.5 us
  other arithmetic: 230 us -> 0 us
  between operations: 125 us -> 0.01 us
  Pallas kernels: 0 us -> 45.6 us
  local copies, waits for them, and re-layouts: 41.1 us -> 2.92 us
  waiting for transfers between devices: 36.5 us -> 0 us
  starting transfers between devices: 10.5 us -> 0 us
    mul x23 -> x0, other arithmetic: 157 us -> none  [the longest x1 115 us: per_device(): return total * (0.25 / (NLAG * NOFF))]
    convert_element_type x80 -> x0, other arithmetic: 50.2 us -> none  [cubic_sum(): pick = (choices_index == indices[offset]).astype(jnp.float32)]
    pallas_call x0 -> x1, Pallas kernels: none -> 45.6 us  [per_device(): pl.pallas_call(functools.partial(kernel, pairs, reach, columns), out_shap...]
    slice x48 -> x0, local copies, waits for them, and re-layouts: 39.5 us -> none  [the longest x40 26.4 us: cubic_sum(): gradient[0] * diff[0] + gradient[1] * diff[1] + gradient[2] * diff[2]]
    ppermute x6 -> x0, waiting for transfers between devices: 36.5 us -> none  [the longest x4 36.5 us: from_behind(): return lax.ppermute(x, axis, [(i, (i + by) % peers) for i in range(peers)])]
    sub x15 -> x0, other arithmetic: 14.7 us -> none  [cubic_sum(): diff = moved.astype(jnp.float32) - base_field]
    ppermute x6 -> x0, starting transfers between devices: 10.5 us -> none  [the longest x4 5.34 us: from_behind(): return lax.ppermute(x, axis, [(i, (i + by) % peers) for i in range(peers)])]
  transfers between devices with their start and end apart: 6 -> 0, of which waited for: 2 -> 0; matrix products, arithmetic and copies ran while one was open for 20% -> 0% of each run, Pallas kernels for 0% -> 0%
where the time goes in v1:
time: 48.7 us; the launch traced here: 48.5 us
  Pallas kernels  45.6 us (94%)
  local copies, waits for them, and re-layouts  2.92 us (6%)
    pallas_call x1, Pallas kernels, per_device(): pl.pallas_call(functools.partial(kernel, pairs, reach, columns), out_shap...  45.6 us
    unnamed x2, local copies, waits for them, and re-layouts  2.92 us

profile of v1, /device:TPU:0, one launch (start us, length us, event | category | flops | bytes accessed | tf_op | source)
XLA Modules:
  0.0 48.5 jit_solution(12798604316780427692)
XLA Ops:
  0.0 1.4 %copy.5.lag_ref = s32[5,3]{1,0:T(8,128)} copy(s32[5,3]{0,1:T(4,128)} %param.5) | data formatting | bytes 120 | tf_op args[1]
  1.4 45.6 %shard_map.46 = f32[16,16,128]{2,1,0:T(8,128)} custom-call(s32[5,3]{1,0:T(8,128)} %copy.5.lag_ref, s32[5,16]{1,0:T(8,128)} %index_ref.1, f32[3,32]{1,0:T(4,128)} %weight_ref.1, bf16[3,16,2,8,128]{4,3,2,1,0:T(8,128)(2,1)} %bitcast.1), custom_call_target="tpu_custom_call" | custom-call | tf_op jit(solution)/shard_map/pallas_call | solution.py:233
  46.9 1.6 %copy.7 = f32[16,16,128]{2,1,0:T(8,128)} copy(f32[16,16,128]{2,1,0:T(8,128)} %shard_map.46) | data formatting | bytes 262144

commit v2 on v1

v2 whole, which is shorter than its diff:
```python
import functools

import jax
import jax.numpy as jnp
from jax import lax
from jax.experimental import pallas as pl
from jax.experimental.pallas import tpu as pltpu
from jax.sharding import PartitionSpec as P

NLAG = 5
NOFF = 16
REACH = 64
YREACH = 4
MESH = pl.DeviceIdType.MESH


def kernel(
    pairs, reach, columns, lag_ref, index_ref, weight_ref, vel_ref, out_ref,
    field, window, matrix, shifts, own_sem, send_sem, recv_sem, share_send, share_recv
):
    tiles, folded = vel_ref.shape[0], vel_ref.shape[2]
    length = vel_ref.shape[4]
    slots = field.shape[0]
    planes, rows = out_ref.shape[0], out_ref.shape[1]
    fold = planes // folded
    strips = matrix.shape[0]
    deep = planes // strips
    high_rows = deep * rows
    order = [0, tiles - 1] + list(range(1, tiles - 1))
    last = tiles + 1
    home = reach % pairs
    me = lax.axis_index("gz")
    col = lax.axis_index("gy")
    pair = me // 2
    side = lax.rem(me, 2)
    up = lax.rem(col + 1, columns)
    down = lax.rem(col + columns - 1, columns)
    partner = (pair * 2 + 1 - side, col)
    others = [s for s in range(slots) if s != home]
    others.sort(key=lambda s: -abs(s - reach))

    def peer(slot):
        return (lax.rem(pair + pairs + reach - slot, pairs) * 2 + side, col)

    own = [
        pltpu.make_async_copy(vel_ref.at[t], field.at[home, side, t + 1], own_sem.at[t])
        for t in order
    ]
    for copy in own:
        copy.start()

    barrier = pltpu.get_barrier_semaphore()
    greeted = [peer(s) for s in others] + [partner, (me, up), (me, down)]
    for device in greeted:
        pl.semaphore_signal(barrier, inc=1, device_id=device, device_id_type=MESH)
    pl.semaphore_wait(barrier, len(greeted))

    def direct(src, slot, tile, device):
        return pltpu.make_async_remote_copy(
            src_ref=src,
            dst_ref=field.at[slot, side, tile],
            send_sem=send_sem.at[slot, tile],
            recv_sem=recv_sem.at[slot, tile],
            device_id=device,
            device_id_type=MESH,
        )

    def share(src, slot, tile):
        return pltpu.make_async_remote_copy(
            src_ref=src,
            dst_ref=field.at[slot, side, tile],
            send_sem=share_send.at[slot, tile],
            recv_sem=share_recv.at[slot, tile],
            device_id=partner,
            device_id_type=MESH,
        )

    def incoming(slot, tile):
        return pltpu.make_async_remote_copy(
            src_ref=field.at[slot, 1 - side, tile],
            dst_ref=field.at[slot, 1 - side, tile],
            send_sem=share_send.at[slot, tile],
            recv_sem=share_recv.at[slot, tile],
            device_id=partner,
            device_id_type=MESH,
        )

    started = []

    def go(copy):
        copy.start()
        started.append(copy)
        return copy

    mains = {}
    halos = {}
    halos[home, 0] = go(direct(vel_ref.at[tiles - 1], home, 0, (me, up)))
    halos[home, last] = go(direct(vel_ref.at[0], home, last, (me, down)))
    for s in others:
        for t in order:
            mains[s, t] = go(direct(vel_ref.at[t], s, t + 1, peer(s)))
    for t in order:
        go(share(vel_ref.at[t], home, t + 1))

    def build(q, _):
        source = lax.broadcasted_iota(jnp.int32, (length, 2 * length), 0)
        column = lax.broadcasted_iota(jnp.int32, (length, 2 * length), 1)
        point = lax.rem(column, length)
        wanted = lax.rem(point + 2 * q + lax.div(column, length), length)
        shifts[q, :length, :] = jnp.where(source == wanted, 1.0, 0.0).astype(jnp.bfloat16)
        shifts[q, length:, :] = jnp.where(source == point, -1.0, 0.0).astype(jnp.bfloat16)
        return 0

    lax.fori_loop(0, NOFF // 2, build, 0)

    for copy in own:
        copy.wait()

    def unfold(i, tile_of, groups):
        for c in range(3):
            for t in groups:
                tile = tile_of(c, t).astype(jnp.float32)
                for f in range(fold):
                    window[c, fold * i + f, t * YREACH:(t + 1) * YREACH, :] = tile[f * YREACH:(f + 1) * YREACH]

    def fill(lag_y, turn, odd, left):
        def strip(m, _):
            for z in range(deep):
                for c in range(3):
                    block = window[c, m * deep + z + odd, pl.ds(YREACH + lag_y, rows), :]
                    if left:
                        block = pltpu.roll(block, turn, 1)
                    at = c * high_rows + z * rows
                    span = slice(0, length) if left else slice(length, 2 * length)
                    matrix[m, at:at + rows, span] = block.astype(jnp.bfloat16)
            if not left:
                out_ref[pl.ds(m * deep, deep)] = jnp.zeros((deep, rows, length), jnp.float32)
            return 0

        lax.fori_loop(0, strips, strip, 0)

    def unfold_home(i, _):
        unfold(i, lambda c, t: field[home, side, t, c, i], range(1, last))
        return 0

    lax.fori_loop(0, folded, unfold_home, 0)
    fill(0, None, 0, False)

    def add_lag(lag, odd):
        turn = lax.rem(length - lag_ref[0, lag], length)
        fill(lag_ref[1, lag], turn, odd, True)

        def step(m, _):
            total = out_ref[pl.ds(m * deep, deep)].reshape(high_rows, length)
            for q in range(NOFF // 2):
                pieces = jnp.dot(matrix[m], shifts[q], preferred_element_type=jnp.float32)
                for h in range(2):
                    row = index_ref[lag, 2 * q + h]
                    g = [weight_ref[c, row] for c in range(3)]
                    diff = [
                        pieces[c * high_rows:(c + 1) * high_rows, h * length:(h + 1) * length]
                        for c in range(3)
                    ]
                    along = g[0] * diff[0] + g[1] * diff[1] + g[2] * diff[2]
                    energy = diff[0] * diff[0] + diff[1] * diff[1] + diff[2] * diff[2]
                    total = total + along * energy
            out_ref[pl.ds(m * deep, deep)] = total.reshape(deep, rows, length)
            return 0

        lax.fori_loop(0, strips, step, 0)

    def end_lag(lag, slot):
        def load(i, _):
            unfold(i, lambda c, t: field[slot, side, t, c, i], range(last + 1))
            return 0

        lax.fori_loop(0, folded, load, 0)
        add_lag(lag, 0)

    def any_lag(lag):
        away = lag_ref[2, lag] + 2 * reach * planes
        odd = lax.rem(away, fold)
        first = lax.div(away, fold)

        def load(i, _):
            block = lax.div(first + i, folded) + side
            place = lax.rem(first + i, folded)
            slot = lax.rem(lax.div(block, 2), pairs)
            parity = lax.rem(block, 2)
            slot = jnp.minimum(slot, slots - 1)
            unfold(i, lambda c, t: field[slot, parity, t, c, place], range(last + 1))
            return 0

        lax.fori_loop(0, folded + 1, load, 0)
        add_lag(lag, odd)

    for s in others:
        for t in order:
            mains[s, t].wait_recv()
            if t == 0:
                halos[s, last] = go(direct(field.at[s, side, 1], s, last, (me, down)))
            if t == tiles - 1:
                halos[s, 0] = go(direct(field.at[s, side, tiles], s, 0, (me, up)))
            go(share(field.at[s, side, t + 1], s, t + 1))
        if s == others[0]:
            for edge in (0, last):
                halos[home, edge].wait_recv()
                go(share(field.at[home, side, edge], home, edge))
    for s in others:
        for edge in (last, 0):
            halos[s, edge].wait_recv()
            go(share(field.at[s, side, edge], s, edge))

    plus = jnp.int32(0)
    minus = jnp.int32(0)
    for lag in range(NLAG - 1, -1, -1):
        plus = jnp.where(lag_ref[2, lag] == REACH, lag, plus)
        minus = jnp.where(lag_ref[2, lag] == -REACH, lag, minus)
    end_lag(plus, (2 * reach) % pairs)
    end_lag(minus, 0)

    for s in [home] + others:
        for t in range(last + 1):
            incoming(s, t).wait_recv()

    low = jnp.minimum(plus, minus)
    high = jnp.maximum(plus, minus)

    def rest(j, _):
        lag = j + jnp.where(j >= low, 1, 0)
        lag = lag + jnp.where(lag >= high, 1, 0)
        any_lag(lag)
        return 0

    lax.fori_loop(0, NLAG - 2, rest, 0)

    def finish(z, _):
        out_ref[z] = out_ref[z] * (0.25 / (NLAG * NOFF))
        return 0

    lax.fori_loop(0, planes, finish, 0)
    for copy in started:
        copy.wait_send()


def solution(mesh):
    count = mesh.shape["gz"]
    columns = mesh.shape["gy"]
    pairs = count // 2

    def per_device(velocity, lag_table, filter_index, filter_weights):
        parts, planes, rows, length = velocity.shape
        reach = REACH // (2 * planes)
        tiles = rows // YREACH
        fold = 8 // YREACH
        strips = max(1, planes * rows // 64)
        slots = min(pairs, 2 * reach + 1)
        blocks = velocity.reshape(parts, planes // fold, fold, tiles, YREACH, length)
        blocks = blocks.transpose(3, 0, 1, 2, 4, 5).reshape(tiles, parts, planes // fold, 8, length)
        smem = pl.BlockSpec(memory_space=pltpu.SMEM)
        return pl.pallas_call(
            functools.partial(kernel, pairs, reach, columns),
            out_shape=jax.ShapeDtypeStruct((planes, rows, length), jnp.float32),
            in_specs=[smem, smem, smem, pl.BlockSpec(memory_space=pl.ANY)],
            out_specs=pl.BlockSpec(memory_space=pltpu.VMEM),
            scratch_shapes=[
                pltpu.VMEM((slots, 2, tiles + 2, parts, planes // fold, 8, length), jnp.bfloat16),
                pltpu.VMEM((parts, planes + fold, rows + 2 * YREACH, length), jnp.float32),
                pltpu.VMEM((strips, parts * planes * rows // strips, 2 * length), jnp.bfloat16),
                pltpu.VMEM((NOFF // 2, 2 * length, 2 * length), jnp.bfloat16),
                pltpu.SemaphoreType.DMA((tiles,)),
                pltpu.SemaphoreType.DMA((slots, tiles + 2)),
                pltpu.SemaphoreType.DMA((slots, tiles + 2)),
                pltpu.SemaphoreType.DMA((slots, tiles + 2)),
                pltpu.SemaphoreType.DMA((slots, tiles + 2)),
            ],
            compiler_params=pltpu.CompilerParams(collective_id=0, has_side_effects=True),
        )(lag_table.T, filter_index, filter_weights, blocks)

    return jax.shard_map(
        per_device,
        mesh=mesh,
        in_specs=(P(None, "gz", "gy", None), P(), P(), P()),
        out_specs=P("gz", "gy", None),
        check_vma=False,
    )
```

time: 48.7 us -> 38.7 us (0.79)
  Pallas kernels: 45.6 us -> 35.3 us
    pallas_call x1, Pallas kernels: 45.6 us -> 35.3 us  [per_device(): pl.pallas_call(functools.partial(kernel, pairs, reach, columns), out_shap...]
    reshape x0 -> x1, local copies, waits for them, and re-layouts: none -> 1.68 us  [per_device(): velocity.reshape(parts, planes // fold, fold, tiles, YREACH, length)]
    unnamed x2 -> x1, local copies, waits for them, and re-layouts: 2.92 us -> 1.57 us
where the time goes in v2:
time: 38.7 us; the launch traced here: 38.5 us
  Pallas kernels  35.3 us (91%)
  local copies, waits for them, and re-layouts  3.25 us (8%)
    pallas_call x1, Pallas kernels, per_device(): pl.pallas_call(functools.partial(kernel, pairs, reach, columns), out_shap...  35.3 us
    reshape x1, local copies, waits for them, and re-layouts, per_device(): velocity.reshape(parts, planes // fold, fold, tiles, YREACH, length)  1.68 us
    unnamed x1, local copies, waits for them, and re-layouts  1.57 us

profile of v2, /device:TPU:0, one launch (start us, length us, event | category | flops | bytes accessed | tf_op | source)
XLA Modules:
  0.0 38.5 jit_solution(14061913217991865066)
XLA Ops:
  0.0 1.7 %copy.5 = bf16[3,8,2,4,4,128]{5,4,2,1,0,3:T(4,128)(2,1)} copy(bf16[3,8,2,4,4,128]{5,4,3,2,1,0:T(4,128)(2,1)} %bitcast.6) | data formatting | bytes 393216 | tf_op jit(solution)/shard_map/reshape | solution.py:258
  1.7 35.3 %shard_map.46 = f32[16,16,128]{2,1,0:T(8,128)} custom-call(s32[3,5]{1,0:T(4,128)} %bitcast.7, s32[5,16]{1,0:T(8,128)} %index_ref.1, f32[3,32]{1,0:T(4,128)} %weight_ref.1, bf16[4,3,8,8,128]{4,3,2,1,0:T(8,128)(2,1)} %bitcast.5), custom_call_target="tpu_custom_call" | custom-call | tf_op jit(solution)/shard_map/pallas_call | solution.py:261
  37.0 1.6 %copy.7 = f32[16,16,128]{2,1,0:T(8,128)} copy(f32[16,16,128]{2,1,0:T(8,128)} %shard_map.46) | data formatting | bytes 262144

commit v3 on v2

--- a/solution.py
+++ b/solution.py
@@ -18,17 +18,15 @@
     pairs, reach, columns, lag_ref, index_ref, weight_ref, vel_ref, out_ref,
     field, window, matrix, shifts, own_sem, send_sem, recv_sem, share_send, share_recv
 ):
-    tiles, folded = vel_ref.shape[0], vel_ref.shape[2]
+    planes, tiles = vel_ref.shape[1], vel_ref.shape[2]
     length = vel_ref.shape[4]
     slots = field.shape[0]
-    planes, rows = out_ref.shape[0], out_ref.shape[1]
-    fold = planes // folded
+    rows = out_ref.shape[1]
     strips = matrix.shape[0]
     deep = planes // strips
     high_rows = deep * rows
     order = [0, tiles - 1] + list(range(1, tiles - 1))
     last = tiles + 1
-    home = reach % pairs
     me = lax.axis_index("gz")
     col = lax.axis_index("gy")
     pair = me // 2
@@ -36,14 +34,31 @@
     up = lax.rem(col + 1, columns)
     down = lax.rem(col + columns - 1, columns)
     partner = (pair * 2 + 1 - side, col)
-    others = [s for s in range(slots) if s != home]
-    others.sort(key=lambda s: -abs(s - reach))
+
+    paired = slots == pairs and pairs & (pairs - 1) == 0 and reach % pairs in (0, pairs // 2)
+    if paired:
+        home = 0
+        ahead = behind = reach % pairs
+        others = sorted(range(1, slots), key=lambda s: (bin(s).count("1"), s != ahead))
+        far = [s for s in others if bin(s).count("1") > 1]
+    else:
+        home, ahead, behind = reach % pairs, (2 * reach) % pairs, 0
+        others = sorted((s for s in range(slots) if s != home), key=lambda s: -abs(s - reach))
+        far = []
+    near = [s for s in others if s not in far]
 
     def peer(slot):
-        return (lax.rem(pair + pairs + reach - slot, pairs) * 2 + side, col)
+        if paired:
+            other = pair
+            for bit in range(pairs.bit_length()):
+                if slot >> bit & 1:
+                    other = other + (1 << bit) - (2 << bit) * lax.rem(pair // (1 << bit), 2)
+        else:
+            other = lax.rem(pair + pairs + reach - slot, pairs)
+        return (other * 2 + side, col)
 
     own = [
-        pltpu.make_async_copy(vel_ref.at[t], field.at[home, side, t + 1], own_sem.at[t])
+        pltpu.make_async_copy(vel_ref.at[:, :, t], field.at[home, side, t + 1], own_sem.at[t])
         for t in order
     ]
     for copy in own:
@@ -92,15 +107,17 @@
         started.append(copy)
         return copy
 
+    for copy in own:
+        copy.wait()
     mains = {}
     halos = {}
-    halos[home, 0] = go(direct(vel_ref.at[tiles - 1], home, 0, (me, up)))
-    halos[home, last] = go(direct(vel_ref.at[0], home, last, (me, down)))
+    halos[home, 0] = go(direct(field.at[home, side, tiles], home, 0, (me, up)))
+    halos[home, last] = go(direct(field.at[home, side, 1], home, last, (me, down)))
     for s in others:
         for t in order:
-            mains[s, t] = go(direct(vel_ref.at[t], s, t + 1, peer(s)))
+            mains[s, t] = go(direct(field.at[home, side, t + 1], s, t + 1, peer(s)))
     for t in order:
-        go(share(vel_ref.at[t], home, t + 1))
+        go(share(field.at[home, side, t + 1], home, t + 1))
 
     def build(q, _):
         source = lax.broadcasted_iota(jnp.int32, (length, 2 * length), 0)
@@ -113,21 +130,16 @@
 
     lax.fori_loop(0, NOFF // 2, build, 0)
 
-    for copy in own:
-        copy.wait()
-
-    def unfold(i, tile_of, groups):
+    def widen(z, tile_of, groups):
         for c in range(3):
             for t in groups:
-                tile = tile_of(c, t).astype(jnp.float32)
-                for f in range(fold):
-                    window[c, fold * i + f, t * YREACH:(t + 1) * YREACH, :] = tile[f * YREACH:(f + 1) * YREACH]
-
-    def fill(lag_y, turn, odd, left):
+                window[c, z, t * YREACH:(t + 1) * YREACH, :] = tile_of(c, t).astype(jnp.float32)
+
+    def fill(lag_y, turn, left):
         def strip(m, _):
             for z in range(deep):
                 for c in range(3):
-                    block = window[c, m * deep + z + odd, pl.ds(YREACH + lag_y, rows), :]
+                    block = window[c, m * deep + z, pl.ds(YREACH + lag_y, rows), :]
                     if left:
                         block = pltpu.roll(block, turn, 1)
                     at = c * high_rows + z * rows
@@ -139,16 +151,16 @@
 
         lax.fori_loop(0, strips, strip, 0)
 
-    def unfold_home(i, _):
-        unfold(i, lambda c, t: field[home, side, t, c, i], range(1, last))
+    def widen_home(z, _):
+        widen(z, lambda c, t: field[home, side, t, c, z], range(1, last))
         return 0
 
-    lax.fori_loop(0, folded, unfold_home, 0)
-    fill(0, None, 0, False)
-
-    def add_lag(lag, odd):
+    lax.fori_loop(0, planes, widen_home, 0)
+    fill(0, None, False)
+
+    def add_lag(lag):
         turn = lax.rem(length - lag_ref[0, lag], length)
-        fill(lag_ref[1, lag], turn, odd, True)
+        fill(lag_ref[1, lag], turn, True)
 
         def step(m, _):
             total = out_ref[pl.ds(m * deep, deep)].reshape(high_rows, length)
@@ -170,31 +182,46 @@
         lax.fori_loop(0, strips, step, 0)
 
     def end_lag(lag, slot):
-        def load(i, _):
-            unfold(i, lambda c, t: field[slot, side, t, c, i], range(last + 1))
+        def load(z, _):
+            widen(z, lambda c, t: field[slot, side, t, c, z], range(last + 1))
             return 0
 
-        lax.fori_loop(0, folded, load, 0)
-        add_lag(lag, 0)
+        lax.fori_loop(0, planes, load, 0)
+        add_lag(lag)
 
     def any_lag(lag):
-        away = lag_ref[2, lag] + 2 * reach * planes
-        odd = lax.rem(away, fold)
-        first = lax.div(away, fold)
-
-        def load(i, _):
-            block = lax.div(first + i, folded) + side
-            place = lax.rem(first + i, folded)
-            slot = lax.rem(lax.div(block, 2), pairs)
+        lag_z = lag_ref[2, lag]
+
+        def load(z, _):
+            away = lag_z + z + 2 * reach * planes
+            block = lax.div(away, planes) + side
+            place = lax.rem(away, planes)
             parity = lax.rem(block, 2)
-            slot = jnp.minimum(slot, slots - 1)
-            unfold(i, lambda c, t: field[slot, parity, t, c, place], range(last + 1))
+            if paired:
+                slot = lax.rem(pair + lax.div(block, 2) + pairs - reach % pairs, pairs) ^ pair
+            else:
+                slot = lax.rem(lax.div(block, 2), pairs)
+            widen(z, lambda c, t: field[slot, parity, t, c, place], range(last + 1))
             return 0
 
-        lax.fori_loop(0, folded + 1, load, 0)
-        add_lag(lag, odd)
-
-    for s in others:
+        lax.fori_loop(0, planes, load, 0)
+        add_lag(lag)
+
+    def pass_halo(s, edge):
+        halos[s, edge].wait_recv()
+        go(share(field.at[s, side, edge], s, edge))
+
+    plus = jnp.int32(0)
+    minus = jnp.int32(0)
+    for lag in range(NLAG - 1, -1, -1):
+        plus = jnp.where(lag_ref[2, lag] == REACH, lag, plus)
+        minus = jnp.where(lag_ref[2, lag] == -REACH, lag, minus)
+
+    for edge in (last, 0):
+        pass_halo(home, edge)
+        for s in far:
+            halos[s, edge] = go(direct(field.at[home, side, edge], s, edge, peer(s)))
+    for s in near:
         for t in order:
             mains[s, t].wait_recv()
             if t == 0:
@@ -202,23 +229,24 @@
             if t == tiles - 1:
                 halos[s, 0] = go(direct(field.at[s, side, tiles], s, 0, (me, up)))
             go(share(field.at[s, side, t + 1], s, t + 1))
-        if s == others[0]:
-            for edge in (0, last):
-                halos[home, edge].wait_recv()
-                go(share(field.at[home, side, edge], home, edge))
-    for s in others:
+    first = near[0]
+    for edge in (last, 0):
+        pass_halo(first, edge)
+    if first == ahead:
+        end_lag(plus, ahead)
+    for s in far:
+        for t in order:
+            mains[s, t].wait_recv()
+            go(share(field.at[s, side, t + 1], s, t + 1))
+    for s in near[1:]:
         for edge in (last, 0):
-            halos[s, edge].wait_recv()
-            go(share(field.at[s, side, edge], s, edge))
-
-    plus = jnp.int32(0)
-    minus = jnp.int32(0)
-    for lag in range(NLAG - 1, -1, -1):
-        plus = jnp.where(lag_ref[2, lag] == REACH, lag, plus)
-        minus = jnp.where(lag_ref[2, lag] == -REACH, lag, minus)
-    end_lag(plus, (2 * reach) % pairs)
-    end_lag(minus, 0)
-
+            pass_halo(s, edge)
+    if first != ahead:
+        end_lag(plus, ahead)
+    end_lag(minus, behind)
+    for s in far:
+        for edge in (last, 0):
+            pass_halo(s, edge)
     for s in [home] + others:
         for t in range(last + 1):
             incoming(s, t).wait_recv()
@@ -252,11 +280,9 @@
         parts, planes, rows, length = velocity.shape
         reach = REACH // (2 * planes)
         tiles = rows // YREACH
-        fold = 8 // YREACH
         strips = max(1, planes * rows // 64)
         slots = min(pairs, 2 * reach + 1)
-        blocks = velocity.reshape(parts, planes // fold, fold, tiles, YREACH, length)
-        blocks = blocks.transpose(3, 0, 1, 2, 4, 5).reshape(tiles, parts, planes // fold, 8, length)
+        blocks = velocity.reshape(parts, planes, tiles, YREACH, length)
         smem = pl.BlockSpec(memory_space=pltpu.SMEM)
         return pl.pallas_call(
             functools.partial(kernel, pairs, reach, columns),
@@ -264,8 +290,8 @@
             in_specs=[smem, smem, smem, pl.BlockSpec(memory_space=pl.ANY)],
             out_specs=pl.BlockSpec(memory_space=pltpu.VMEM),
             scratch_shapes=[
-                pltpu.VMEM((slots, 2, tiles + 2, parts, planes // fold, 8, length), jnp.bfloat16),
-                pltpu.VMEM((parts, planes + fold, rows + 2 * YREACH, length), jnp.float32),
+                pltpu.VMEM((slots, 2, tiles + 2, parts, planes, YREACH, length), jnp.bfloat16),
+                pltpu.VMEM((parts, planes, rows + 2 * YREACH, length), jnp.float32),
                 pltpu.VMEM((strips, parts * planes * rows // strips, 2 * length), jnp.bfloat16),
                 pltpu.VMEM((NOFF // 2, 2 * length, 2 * length), jnp.bfloat16),
                 pltpu.SemaphoreType.DMA((tiles,)),

time: 38.7 us -> 31.8 us (0.82)
  the two profiles are of different devices: /device:TPU:0 before, /device:TPU:1 now
where the time goes in v3:
time: 31.8 us; the launch traced here: 31.6 us
  Pallas kernels  30 us (94%)
  local copies, waits for them, and re-layouts  1.57 us (5%)
    pallas_call x1, Pallas kernels, per_device(): pl.pallas_call(functools.partial(kernel, pairs, reach, columns), out_shap...  30 us
    unnamed x1, local copies, waits for them, and re-layouts  1.57 us

profile of v3, /device:TPU:1, one launch (start us, length us, event | category | flops | bytes accessed | tf_op | source)
XLA Modules:
  0.0 31.6 jit_solution(15324276802449185507)
XLA Ops:
  0.0 30.0 %shard_map.46 = f32[16,16,128]{2,1,0:T(8,128)} custom-call(s32[3,5]{1,0:T(4,128)} %bitcast.3, s32[5,16]{1,0:T(8,128)} %index_ref.1, f32[3,32]{1,0:T(4,128)} %weight_ref.1, bf16[3,16,4,4,128]{4,3,2,1,0:T(4,128)(2,1)} %bitcast.2), custom_call_target="tpu_custom_call" | custom-call | tf_op jit(solution)/shard_map/pallas_call | solution.py:287
  30.1 1.6 %copy.6 = f32[16,16,128]{2,1,0:T(8,128)} copy(f32[16,16,128]{2,1,0:T(8,128)} %shard_map.46) | data formatting | bytes 262144

commit v4 on v3

--- a/solution.py
+++ b/solution.py
@@ -22,7 +22,7 @@
     length = vel_ref.shape[4]
     slots = field.shape[0]
     rows = out_ref.shape[1]
-    strips = matrix.shape[0]
+    strips = matrix.shape[1]
     deep = planes // strips
     high_rows = deep * rows
     order = [0, tiles - 1] + list(range(1, tiles - 1))
@@ -46,6 +46,9 @@
         others = sorted((s for s in range(slots) if s != home), key=lambda s: -abs(s - reach))
         far = []
     near = [s for s in others if s not in far]
+    relayed = None
+    if len(far) == 1 and len(near) == 2:
+        relayed = {near[0]: range(tiles // 2), near[1]: range(tiles // 2, tiles)}
 
     def peer(slot):
         if paired:
@@ -113,8 +116,8 @@
     halos = {}
     halos[home, 0] = go(direct(field.at[home, side, tiles], home, 0, (me, up)))
     halos[home, last] = go(direct(field.at[home, side, 1], home, last, (me, down)))
-    for s in others:
-        for t in order:
+    for t in order:
+        for s in near if relayed else others:
             mains[s, t] = go(direct(field.at[home, side, t + 1], s, t + 1, peer(s)))
     for t in order:
         go(share(field.at[home, side, t + 1], home, t + 1))
@@ -135,77 +138,69 @@
             for t in groups:
                 window[c, z, t * YREACH:(t + 1) * YREACH, :] = tile_of(c, t).astype(jnp.float32)
 
-    def fill(lag_y, turn, left):
-        def strip(m, _):
-            for z in range(deep):
-                for c in range(3):
-                    block = window[c, m * deep + z, pl.ds(YREACH + lag_y, rows), :]
-                    if left:
-                        block = pltpu.roll(block, turn, 1)
-                    at = c * high_rows + z * rows
-                    span = slice(0, length) if left else slice(length, 2 * length)
-                    matrix[m, at:at + rows, span] = block.astype(jnp.bfloat16)
-            if not left:
-                out_ref[pl.ds(m * deep, deep)] = jnp.zeros((deep, rows, length), jnp.float32)
-            return 0
-
-        lax.fori_loop(0, strips, strip, 0)
-
     def widen_home(z, _):
         widen(z, lambda c, t: field[home, side, t, c, z], range(1, last))
         return 0
 
     lax.fori_loop(0, planes, widen_home, 0)
-    fill(0, None, False)
-
-    def add_lag(lag):
-        turn = lax.rem(length - lag_ref[0, lag], length)
-        fill(lag_ref[1, lag], turn, True)
-
-        def step(m, _):
-            total = out_ref[pl.ds(m * deep, deep)].reshape(high_rows, length)
-            for q in range(NOFF // 2):
-                pieces = jnp.dot(matrix[m], shifts[q], preferred_element_type=jnp.float32)
-                for h in range(2):
-                    row = index_ref[lag, 2 * q + h]
-                    g = [weight_ref[c, row] for c in range(3)]
-                    diff = [
-                        pieces[c * high_rows:(c + 1) * high_rows, h * length:(h + 1) * length]
-                        for c in range(3)
-                    ]
-                    along = g[0] * diff[0] + g[1] * diff[1] + g[2] * diff[2]
-                    energy = diff[0] * diff[0] + diff[1] * diff[1] + diff[2] * diff[2]
-                    total = total + along * energy
-            out_ref[pl.ds(m * deep, deep)] = total.reshape(deep, rows, length)
+
+    def fill_home(m, _):
+        for z in range(deep):
+            for c in range(3):
+                block = window[c, m * deep + z, YREACH:YREACH + rows, :].astype(jnp.bfloat16)
+                at = c * high_rows + z * rows
+                for buffer in range(2):
+                    matrix[buffer, m, at:at + rows, length:] = block
+        out_ref[pl.ds(m * deep, deep)] = jnp.zeros((deep, rows, length), jnp.float32)
+        return 0
+
+    lax.fori_loop(0, strips, fill_home, 0)
+
+    def end_plane(slot):
+        return lambda lag, z: (lambda c, t: field[slot, side, t, c, z])
+
+    def any_plane(lag, z):
+        away = lag_ref[2, lag] + z + 2 * reach * planes
+        block = lax.div(away, planes) + side
+        place = lax.rem(away, planes)
+        parity = lax.rem(block, 2)
+        if paired:
+            slot = lax.rem(pair + lax.div(block, 2) + pairs - reach % pairs, pairs) ^ pair
+        else:
+            slot = lax.rem(lax.div(block, 2), pairs)
+        return lambda c, t: field[slot, parity, t, c, place]
+
+    def sweep(work, ahead_work, buffer):
+        def strip(m, _):
+            if ahead_work is not None:
+                later, plane_of = ahead_work
+                turn = lax.rem(length - lag_ref[0, later], length)
+                lag_y = lag_ref[1, later]
+                for z in range(deep):
+                    widen(m * deep + z, plane_of(later, m * deep + z), range(last + 1))
+                for z in range(deep):
+                    for c in range(3):
+                        block = window[c, m * deep + z, pl.ds(YREACH + lag_y, rows), :]
+                        at = c * high_rows + z * rows
+                        matrix[1 - buffer, m, at:at + rows, :length] = pltpu.roll(block, turn, 1).astype(jnp.bfloat16)
+            if work is not None:
+                total = out_ref[pl.ds(m * deep, deep)].reshape(high_rows, length)
+                for q in range(NOFF // 2):
+                    pieces = jnp.dot(matrix[buffer, m], shifts[q], preferred_element_type=jnp.float32)
+                    for h in range(2):
+                        row = index_ref[work, 2 * q + h]
+                        g = [weight_ref[c, row] for c in range(3)]
+                        diff = [
+                            pieces[c * high_rows:(c + 1) * high_rows, h * length:(h + 1) * length]
+                            for c in range(3)
+                        ]
+                        along = g[0] * diff[0] + g[1] * diff[1] + g[2] * diff[2]
+                        energy = diff[0] * diff[0] + diff[1] * diff[1] + diff[2] * diff[2]
+                        total = total + along * energy
+                out_ref[pl.ds(m * deep, deep)] = total.reshape(deep, rows, length)
             return 0
 
-        lax.fori_loop(0, strips, step, 0)
-
-    def end_lag(lag, slot):
-        def load(z, _):
-            widen(z, lambda c, t: field[slot, side, t, c, z], range(last + 1))
-            return 0
-
-        lax.fori_loop(0, planes, load, 0)
-        add_lag(lag)
-
-    def any_lag(lag):
-        lag_z = lag_ref[2, lag]
-
-        def load(z, _):
-            away = lag_z + z + 2 * reach * planes
-            block = lax.div(away, planes) + side
-            place = lax.rem(away, planes)
-            parity = lax.rem(block, 2)
-            if paired:
-                slot = lax.rem(pair + lax.div(block, 2) + pairs - reach % pairs, pairs) ^ pair
-            else:
-                slot = lax.rem(lax.div(block, 2), pairs)
-            widen(z, lambda c, t: field[slot, parity, t, c, place], range(last + 1))
-            return 0
-
-        lax.fori_loop(0, planes, load, 0)
-        add_lag(lag)
+        lax.fori_loop(0, strips, strip, 0)
 
     def pass_halo(s, edge):
         halos[s, edge].wait_recv()
@@ -217,33 +212,41 @@
         plus = jnp.where(lag_ref[2, lag] == REACH, lag, plus)
         minus = jnp.where(lag_ref[2, lag] == -REACH, lag, minus)
 
+    def pass_main(s, t):
+        mains[s, t].wait_recv()
+        if t == 0:
+            halos[s, last] = go(direct(field.at[s, side, 1], s, last, (me, down)))
+        if t == tiles - 1:
+            halos[s, 0] = go(direct(field.at[s, side, tiles], s, 0, (me, up)))
+        if relayed and t in relayed[s]:
+            mains[far[0], t] = go(direct(field.at[s, side, t + 1], far[0], t + 1, peer(far[0] ^ s)))
+        go(share(field.at[s, side, t + 1], s, t + 1))
+
+    for t in order[:2]:
+        for s in near:
+            pass_main(s, t)
     for edge in (last, 0):
         pass_halo(home, edge)
         for s in far:
             halos[s, edge] = go(direct(field.at[home, side, edge], s, edge, peer(s)))
-    for s in near:
-        for t in order:
-            mains[s, t].wait_recv()
-            if t == 0:
-                halos[s, last] = go(direct(field.at[s, side, 1], s, last, (me, down)))
-            if t == tiles - 1:
-                halos[s, 0] = go(direct(field.at[s, side, tiles], s, 0, (me, up)))
-            go(share(field.at[s, side, t + 1], s, t + 1))
-    first = near[0]
-    for edge in (last, 0):
-        pass_halo(first, edge)
-    if first == ahead:
-        end_lag(plus, ahead)
+    for t in order[2:]:
+        for s in near:
+            pass_main(s, t)
+    early = [ahead] if ahead == behind else near
+    for s in early:
+        for edge in (last, 0):
+            pass_halo(s, edge)
+    sweep(None, (plus, end_plane(ahead)), 1)
+    sweep(plus, (minus, end_plane(behind)), 0)
     for s in far:
         for t in order:
             mains[s, t].wait_recv()
             go(share(field.at[s, side, t + 1], s, t + 1))
-    for s in near[1:]:
-        for edge in (last, 0):
-            pass_halo(s, edge)
-    if first != ahead:
-        end_lag(plus, ahead)
-    end_lag(minus, behind)
+    for s in near:
+        if s not in early:
+            for edge in (last, 0):
+                pass_halo(s, edge)
+    sweep(minus, None, 1)
     for s in far:
         for edge in (last, 0):
             pass_halo(s, edge)
@@ -254,13 +257,12 @@
     low = jnp.minimum(plus, minus)
     high = jnp.maximum(plus, minus)
 
-    def rest(j, _):
+    rest = []
+    for j in range(NLAG - 2):
         lag = j + jnp.where(j >= low, 1, 0)
-        lag = lag + jnp.where(lag >= high, 1, 0)
-        any_lag(lag)
-        return 0
-
-    lax.fori_loop(0, NLAG - 2, rest, 0)
+        rest.append((lag + jnp.where(lag >= high, 1, 0), any_plane))
+    for j, work in enumerate([None] + rest):
+        sweep(None if work is None else work[0], rest[j] if j < len(rest) else None, (j + 1) % 2)
 
     def finish(z, _):
         out_ref[z] = out_ref[z] * (0.25 / (NLAG * NOFF))
@@ -292,7 +294,7 @@
             scratch_shapes=[
                 pltpu.VMEM((slots, 2, tiles + 2, parts, planes, YREACH, length), jnp.bfloat16),
                 pltpu.VMEM((parts, planes, rows + 2 * YREACH, length), jnp.float32),
-                pltpu.VMEM((strips, parts * planes * rows // strips, 2 * length), jnp.bfloat16),
+                pltpu.VMEM((2, strips, parts * planes * rows // strips, 2 * length), jnp.bfloat16),
                 pltpu.VMEM((NOFF // 2, 2 * length, 2 * length), jnp.bfloat16),
                 pltpu.SemaphoreType.DMA((tiles,)),
                 pltpu.SemaphoreType.DMA((slots, tiles + 2)),

time: 31.8 us -> 28.8 us (0.906)
  Pallas kernels: 30 us -> 27.1 us
    pallas_call x1, Pallas kernels: 30 us -> 27.1 us  [per_device(): pl.pallas_call(functools.partial(kernel, pairs, reach, columns), out_shap...]
where the time goes in v4:
time: 28.8 us; the launch traced here: 28.7 us
  Pallas kernels  27.1 us (94%)
  local copies, waits for them, and re-layouts  1.57 us (5%)
    pallas_call x1, Pallas kernels, per_device(): pl.pallas_call(functools.partial(kernel, pairs, reach, columns), out_shap...  27.1 us
    unnamed x1, local copies, waits for them, and re-layouts  1.57 us

profile of v4, /device:TPU:1, one launch (start us, length us, event | category | flops | bytes accessed | tf_op | source)
XLA Modules:
  0.0 28.7 jit_solution(5812812399948004568)
XLA Ops:
  0.0 27.1 %shard_map.46 = f32[16,16,128]{2,1,0:T(8,128)} custom-call(s32[3,5]{1,0:T(4,128)} %bitcast.3, s32[5,16]{1,0:T(8,128)} %index_ref.1, f32[3,32]{1,0:T(4,128)} %weight_ref.1, bf16[3,16,4,4,128]{4,3,2,1,0:T(4,128)(2,1)} %bitcast.2), custom_call_target="tpu_custom_call" | custom-call | tf_op jit(solution)/shard_map/pallas_call | solution.py:289
  27.1 1.6 %copy.6 = f32[16,16,128]{2,1,0:T(8,128)} copy(f32[16,16,128]{2,1,0:T(8,128)} %shard_map.46) | data formatting | bytes 262144

commit v5 on v4

--- a/solution.py
+++ b/solution.py
@@ -170,7 +170,7 @@
             slot = lax.rem(lax.div(block, 2), pairs)
         return lambda c, t: field[slot, parity, t, c, place]
 
-    def sweep(work, ahead_work, buffer):
+    def sweep(work, ahead_work, buffer, scale=None):
         def strip(m, _):
             if ahead_work is not None:
                 later, plane_of = ahead_work
@@ -197,6 +197,8 @@
                         along = g[0] * diff[0] + g[1] * diff[1] + g[2] * diff[2]
                         energy = diff[0] * diff[0] + diff[1] * diff[1] + diff[2] * diff[2]
                         total = total + along * energy
+                if scale is not None:
+                    total = total * scale
                 out_ref[pl.ds(m * deep, deep)] = total.reshape(deep, rows, length)
             return 0
 
@@ -246,10 +248,10 @@
         if s not in early:
             for edge in (last, 0):
                 pass_halo(s, edge)
-    sweep(minus, None, 1)
     for s in far:
         for edge in (last, 0):
             pass_halo(s, edge)
+    sweep(minus, None, 1)
     for s in [home] + others:
         for t in range(last + 1):
             incoming(s, t).wait_recv()
@@ -262,13 +264,9 @@
         lag = j + jnp.where(j >= low, 1, 0)
         rest.append((lag + jnp.where(lag >= high, 1, 0), any_plane))
     for j, work in enumerate([None] + rest):
-        sweep(None if work is None else work[0], rest[j] if j < len(rest) else None, (j + 1) % 2)
-
-    def finish(z, _):
-        out_ref[z] = out_ref[z] * (0.25 / (NLAG * NOFF))
-        return 0
-
-    lax.fori_loop(0, planes, finish, 0)
+        scale = 0.25 / (NLAG * NOFF) if j == len(rest) else None
+        sweep(None if work is None else work[0], rest[j] if j < len(rest) else None, (j + 1) % 2, scale)
+
     for copy in started:
         copy.wait_send()
 

time: 28.8 us -> 28 us (0.972)
  the two profiles are of different devices: /device:TPU:1 before, /device:TPU:0 now
where the time goes in v5:
time: 28 us; the launch traced here: 27.8 us
  Pallas kernels  26.3 us (94%)
  local copies, waits for them, and re-layouts  1.57 us (6%)
    pallas_call x1, Pallas kernels, per_device(): pl.pallas_call(functools.partial(kernel, pairs, reach, columns), out_shap...  26.3 us
    unnamed x1, local copies, waits for them, and re-layouts  1.57 us

profile of v5, /device:TPU:0, one launch (start us, length us, event | category | flops | bytes accessed | tf_op | source)
XLA Modules:
  0.0 27.8 jit_solution(17440202712037221194)
XLA Ops:
  0.0 26.3 %shard_map.46 = f32[16,16,128]{2,1,0:T(8,128)} custom-call(s32[3,5]{1,0:T(4,128)} %bitcast.3, s32[5,16]{1,0:T(8,128)} %index_ref.1, f32[3,32]{1,0:T(4,128)} %weight_ref.1, bf16[3,16,4,4,128]{4,3,2,1,0:T(4,128)(2,1)} %bitcast.2), custom_call_target="tpu_custom_call" | custom-call | tf_op jit(solution)/shard_map/pallas_call | solution.py:287
  26.3 1.6 %copy.6 = f32[16,16,128]{2,1,0:T(8,128)} copy(f32[16,16,128]{2,1,0:T(8,128)} %shard_map.46) | data formatting | bytes 262144
